TPU v7x, 32 devices: a whole 2x2x4 slice. The times are simulated.
32 devices in a mesh: parts: 2 (over y), src: 4 (over z), tile: 2 (over x), row: 2 (over core).
Axes of the slice: x: 2, y: 2, z: 4, core: 2. Of those that a mesh axis runs over, the one named last changes fastest.
Arguments:
- mask_windows: float32 [4, 256, 256], P(('parts', 'tile'), ('src', 'row')), parts along dimension 0, may hold values from -4 to 4
- target_windows: float32 [4, 256, 256], P(('parts', 'tile'), ('src', 'row')), parts along dimension 0, may hold values from 0 to 1
- pupil_bands: int32 [24, 128, 2], P(('parts', 'src')), parts along dimension 0, may hold values from 0 to 128, as said below
- pupil_phase: float32 [24, 128, 128], P(('parts', 'src')), parts along dimension 0, may hold values from -3.140625 to 3.140625
- source_weight: float32 [24], P(('parts', 'src')), parts along dimension 0, may hold values from 0.2 to 1
Outputs:
- mask_grad: float32 [4, 256, 256], P(('parts', 'tile'), ('src', 'row')), parts along dimension 0
- source_grad: float32 [24], P(('parts', 'src')), parts along dimension 0
There are 2 independent parts, one for each index of `parts`. A program takes and returns all parts, laid end to end along the dimension named above; each array names one. Nothing has to cross between parts.
Inputs may be any that keep to these rules, and one draw needn't show every extreme that they name: For every source point and frequency row, pupil_bands[s, kx, 0] <= pupil_bands[s, kx, 1]; a row that passes nothing holds (0, 0).
All inputs are finite; a program needn't handle non-finite values.
Results may differ from a plain program's by a relative error of at most 0.00019.
Values sent between devices are 32-bit elements; how exact they have to be, the bound alone decides.
A program may use at most 64 MiB of HBM per device.

v0:
```python
import math

import jax
import jax.numpy as jnp
from jax import lax
from jax.sharding import PartitionSpec as P

M = 256
K = 128
OV = 32


STEEPNESS = 20.0
THRESHOLD = 0.15
LOSS_SCALE = 32.0


def with_halo(block, sides, width):
    for axis, dim in sides:
        count = lax.axis_size(axis)
        forward = [(i, i + 1) for i in range(count - 1)]
        backward = [(target, source) for source, target in forward]
        low = lax.ppermute(
            lax.slice_in_dim(block, block.shape[dim] - width, None, axis=dim), axis, forward
        )
        high = lax.ppermute(lax.slice_in_dim(block, 0, width, axis=dim), axis, backward)
        block = jnp.concatenate([low, block, high], axis=dim)
    return block


def matmul(left_op, right_op):
    return lax.dot_general(
        left_op,
        right_op,
        (((1,), (0,)), ((), ())),
        precision=lax.Precision.HIGHEST,
        preferred_element_type=jnp.float32,
    )


def matmul_tn(left_op, right_op):
    return lax.dot_general(
        left_op,
        right_op,
        (((0,), (0,)), ((), ())),
        precision=lax.Precision.HIGHEST,
        preferred_element_type=jnp.float32,
    )


def matmul_nt(left_op, right_op):
    return lax.dot_general(
        left_op,
        right_op,
        (((1,), (1,)), ((), ())),
        precision=lax.Precision.HIGHEST,
        preferred_element_type=jnp.float32,
    )


def wave_tables(positions):
    freq_index = jnp.arange(K, dtype=jnp.int32) - K // 2
    phase_index = freq_index[:, None] * positions[None, :] % M
    angles = 2.0 * math.pi / M * phase_index.astype(jnp.float32)
    return (jnp.cos(angles), jnp.sin(angles))


def shards(mask_windows, target_windows, pupil_bands, pupil_phase, source_weight):
    src_count = lax.axis_size("src")
    tile_count = lax.axis_size("tile")
    row_count = lax.axis_size("row")
    local_x = mask_windows.shape[1]
    per_device = pupil_phase.shape[0]
    sources = per_device * src_count
    field_scale = 1.0 / (M * K)
    src_id = lax.axis_index("src")
    row_id = lax.axis_index("row")
    x_start = (src_id * row_count + row_id) * local_x
    block_starts = (jnp.arange(src_count, dtype=jnp.int32) * row_count + row_id) * local_x
    row_set = (block_starts[:, None] + jnp.arange(local_x, dtype=jnp.int32)[None, :]).reshape(
        src_count * local_x
    )
    cos_all, sin_all = wave_tables(jnp.arange(M, dtype=jnp.int32))
    cos_set, sin_set = wave_tables(row_set)
    cos_own, sin_own = wave_tables(x_start + jnp.arange(local_x, dtype=jnp.int32))
    window = mask_windows[0]
    goal_block = target_windows[0]
    zero_spec = jnp.zeros((K, K), jnp.float32)
    shard_rows = lax.all_gather(window, ("src", "row"), axis=0, tiled=True)
    part_real = matmul_nt(shard_rows, cos_all)
    part_imag = -matmul_nt(shard_rows, sin_all)
    spec_real = matmul(cos_all, part_real) + matmul(sin_all, part_imag)
    spec_imag = matmul(cos_all, part_imag) - matmul(sin_all, part_real)
    freq_cols = jnp.arange(K, dtype=jnp.int32)
    inside = (freq_cols[None, None, :] >= pupil_bands[:, :, 0:1]) & (
        freq_cols[None, None, :] < pupil_bands[:, :, 1:2]
    )
    passing = inside.astype(jnp.float32)
    pupil_real = passing * jnp.cos(pupil_phase)
    pupil_imag = passing * jnp.sin(pupil_phase)
    amp_real = (pupil_real * spec_real - pupil_imag * spec_imag).reshape(per_device * K, K)
    amp_imag = (pupil_imag * spec_real + pupil_real * spec_imag).reshape(per_device * K, K)
    half_real = (matmul(amp_real, cos_all) - matmul(amp_imag, sin_all)).reshape(per_device, K, M)
    half_imag = (matmul(amp_real, sin_all) + matmul(amp_imag, cos_all)).reshape(per_device, K, M)
    weights = source_weight / sources

    def fields(pair_in):
        one_real, one_imag = pair_in
        field_real = field_scale * (matmul_tn(cos_set, one_real) - matmul_tn(sin_set, one_imag))
        field_imag = field_scale * (matmul_tn(cos_set, one_imag) + matmul_tn(sin_set, one_real))
        return (field_real, field_imag)

    stack_real, stack_imag = lax.map(fields, (half_real, half_imag))
    part_real = stack_real
    part_imag = stack_imag
    intensity = lax.psum_scatter(
        jnp.sum(weights[:, None, None] * (part_real * part_real + part_imag * part_imag), axis=0),
        "src",
        scatter_dimension=0,
        tiled=True,
    )
    resist = jax.nn.sigmoid(STEEPNESS * (intensity - THRESHOLD))
    cotangent = LOSS_SCALE * (resist - goal_block) * STEEPNESS * resist * (1.0 - resist)
    cotangent_all = lax.all_gather(cotangent, "src", axis=0, tiled=True)
    source_ids = jnp.arange(per_device, dtype=jnp.int32)

    def add_back(source_id, totals):
        grad_real, grad_imag, source_terms = totals
        field_real = stack_real[source_id]
        field_imag = stack_imag[source_id]
        back_scale = 2.0 * weights[source_id] * cotangent_all
        back_real = back_scale * field_real
        back_imag = back_scale * field_imag
        adj_real = matmul(cos_set, back_real) + matmul(sin_set, back_imag)
        adj_imag = matmul(cos_set, back_imag) - matmul(sin_set, back_real)
        amp_grad_real = field_scale * (matmul_nt(adj_real, cos_all) + matmul_nt(adj_imag, sin_all))
        amp_grad_imag = field_scale * (matmul_nt(adj_imag, cos_all) - matmul_nt(adj_real, sin_all))
        pass_real = pupil_real[source_id]
        pass_imag = pupil_imag[source_id]
        grad_real = grad_real + pass_real * amp_grad_real + pass_imag * amp_grad_imag
        grad_imag = grad_imag + pass_real * amp_grad_imag - pass_imag * amp_grad_real
        term_value = jnp.sum(cotangent_all * (field_real * field_real + field_imag * field_imag))
        source_terms = source_terms + jnp.where(source_ids == source_id, term_value, 0.0)
        return (grad_real, grad_imag, source_terms)

    grad_real, grad_imag, source_terms = lax.fori_loop(
        0, per_device, add_back, (zero_spec, zero_spec, jnp.zeros((per_device,), jnp.float32))
    )
    grad_real, grad_imag = lax.psum((grad_real, grad_imag), ("src", "row"))
    source_sum = lax.psum(source_terms, ("tile", "row"))
    source_grad = source_sum / (sources * M * tile_count)
    q_one = matmul(grad_real, cos_all) - matmul(grad_imag, sin_all)
    q_two = matmul(grad_real, sin_all) + matmul(grad_imag, cos_all)
    grad_block = matmul_tn(cos_own, q_one) - matmul_tn(sin_own, q_two)
    padded = with_halo(grad_block, (("tile", 1),), OV)
    from_below = padded[:, :OV]
    from_above = padded[:, M + OV :]
    middle = jnp.zeros((local_x, M - 2 * OV), jnp.float32)
    grad_block = grad_block + jnp.concatenate([from_below, middle, from_above], axis=1)
    return (grad_block[None], source_grad)


def solution(mesh):
    return jax.shard_map(
        shards,
        mesh=mesh,
        in_specs=(
            P(("parts", "tile"), ("src", "row"), None),
            P(("parts", "tile"), ("src", "row"), None),
            P(("parts", "src"), None, None),
            P(("parts", "src"), None, None),
            P(("parts", "src")),
        ),
        out_specs=(P(("parts", "tile"), ("src", "row"), None), P(("parts", "src"))),
        check_vma=False,
    )
```

profile of v0, /device:TPU:0, one launch (start us, length us, event | category | flops | bytes accessed | tf_op | source)
XLA Modules:
  0.0 179.0 jit_solution(342020758289789825)
XLA Ops:
  7.2 16.1 %all-gather = f32[1,256,256]{2,1,0:T(8,128)S(1)} all-gather(f32[1,32,256]{2,1,0:T(8,128)} %param.9), channel_id=2, replica_groups=mesh['parts'=2,'src'=4,'tile'=2,'row'=2] {'src','row'}, dimensions={1}, use_global_device_ids=true | all-gather | bytes 294912 | tf_op jit(solution)/shard_map/all_gather | solution.py:89
  23.3 0.9 fusion.123
  24.2 0.9 convolution_negate_fusion
  29.3 1.0 fusion.152
  30.3 1.0 fusion.142
  31.3 1.0 convolution_add_fusion.3
  32.4 1.0 convolution_subtract_fusion.3
  33.6 7.2 %while.35 = (s32[]{:T(128)}, f32[3,128,256]{1,2,0:T(8,128)S(1)}, f32[3,128,256]{1,2,0:T(8,128)S(1)}, f32[3,128,256]{2,1,0:T(8,128)S(1)}, f32[3,128,256]{2,1,0:T(...) while((s32[]{:T(128)}, f32[3,128,256]{1,2,0:T(8,128)S(1)}, ...), condition=%wide.region_1.2_spmd.clone.clone, body=%wide.region_0.1_spmd.clone.clone.sunk | while | flops 202375168 | bytes 1316957 | solution.py:113
  41.9 20.5 %reduce-scatter.4.cloned.1.call-done = f32[32,256]{1,0:T(8,128)} async-done(((f32[128,256]{1,0:T(8,128)}), f32[32,256]{1,0:T(8,128)}) %reduce-scatter.4.cloned.1.call-update) | async-done | bytes 32784 | tf_op jit(solution)/shard_map/reduce_scatter | solution.py:116
  63.1 13.5 %all_gather.7 = f32[128,256]{1,0:T(8,128)S(1)} all-gather(f32[32,256]{1,0:T(8,128)S(1)} %fusion.163), channel_id=1, replica_groups=mesh['parts'=2,'src'=4,'tile'=2,'row'=2] {'src'}, dimensions={0}, use_global_device_ids=true | all-gather | bytes 163840 | tf_op jit(solution)/shard_map/all_gather | solution.py:124
  76.7 26.2 %while.36 = (s32[]{:T(128)}, f32[128,128]{1,0:T(8,128)S(1)}, f32[128,128]{1,0:T(8,128)S(1)}, f32[3]{0:T(128)S(1)}, f32[3,128,128]{2,1,0:T(8,128)S(1)}, /*index=5...) while((s32[]{:T(128)}, f32[128,128]{1,0:T(8,128)S(1)}, ...), condition=%wide.region_6.7_spmd.clone.clone.clone.clone, body=%wide.region_4.6_spmd.clone.clone.clone.clone.sunk | while | flops 406126592 | bytes 4593900 | solution.py:146
  81.5 0.8 fusion.307
  82.3 0.8 fusion.308
  83.2 0.9 fusion.309
  90.2 0.8 fusion.307
  91.9 0.9 fusion.309
  98.9 0.9 fusion.307
  100.7 0.9 fusion.309
  103.5 5.7 %psum.23 = f32[3]{0:T(128)S(1)} all-reduce(f32[3]{0:T(128)S(1)} %get-tuple-element.296), channel_id=1, replica_groups=mesh['parts'=2,'src'=4,'tile'=2,'row'=2] {'tile','row'}, use_global_device_ids=true, to_apply=%region_9.10 | all-reduce | flops 3 | bytes 24 | tf_op jit(solution)/shard_map/psum | solution.py:150
  109.2 47.8 %all-reduce.3.cloned.1.call-done = (f32[128,128]{1,0:T(8,128)}, f32[128,128]{1,0:T(8,128)}) async-done(((f32[128,128]{1,0:T(8,128)}, f32[128,128]{1,0:T(8,128)}), (f32[128,128]{1,0:T(8,128)}, f32[128,128]{1,0:T(8,128)})) %all-reduce.3.cloned.1.call-update) | async-done | bytes 131088 | tf_op jit(solution)/shard_map/psum | solution.py:149
  157.1 1.7 fusion.150
  162.5 3.4 %collective-permute-start = (f32[32,32]{1,0:T(8,128)S(1)}, f32[32,32]{1,0:T(8,128)S(1)}, u32[]{:S(2)}, u32[]{:S(2)}) collective-permute-start(f32[32,32]{1,0:T(8,128)S(1)} %get-tuple-element.617), channel_id=1, source_target_pairs={{0,2},{1,3},{4,6},{5,7},{8,10},{9,11},{12,14},{13,15},{16,18},{17,... | collective-permute-start | bytes 12296 | tf_op jit(solution)/shard_map/ppermute | solution.py:23
  165.9 1.3 collective-permute-start.1
  167.7 3.8 %collective-permute-done.1 = f32[32,32]{1,0:T(8,128)S(1)} collective-permute-done((f32[32,32]{1,0:T(8,128)S(1)}, f32[32,32]{1,0:T(8,128)S(1)}, u32[]{:S(2)}, u32[]{:S(2)}) %collective-permute-start.1) | collective-permute-done | bytes 4128 | tf_op jit(solution)/shard_map/ppermute | solution.py:26
  (100 shorter events, 36.6 us)
Async XLA Ops:
  7.2 55.2 %reduce-scatter.4.cloned.1.call-start = ((), (), s32[]{:S(2)}) async-start(), calls=%async_computation.1 | async-start | bytes 163840 | tf_op jit(solution)/shard_map/reduce_scatter | solution.py:116
  27.5 0.8 copy-start.4
  27.6 0.9 copy-start
  33.6 7.2 %copy-start.7 = (f32[3]{0:T(128)S(1)}, f32[3]{0:T(128)}, u32[]{:S(2)}) copy-start(f32[3]{0:T(128)} %param.13) | copy-start | bytes 40
  41.7 20.7 %copy-start.3 = (f32[1,32,256]{2,1,0:T(8,128)S(1)}, f32[1,32,256]{2,1,0:T(8,128)}, u32[]{:S(2)}) copy-start(f32[1,32,256]{2,1,0:T(8,128)} %param.10) | copy-start | bytes 98308
  41.7 115.4 %all-reduce.3.cloned.1.call-start = ((), (), s32[]{:S(2)}) async-start(), calls=%async_computation.2 | async-start | bytes 262144 | tf_op jit(solution)/shard_map/psum | solution.py:149
  102.8 0.6 copy-start.1
  102.9 0.6 copy-start.2
  157.1 1.7 copy-start.6
  158.8 0.8 copy-start.5
  162.5 5.2 %collective-permute-start = (f32[32,32]{1,0:T(8,128)S(1)}, f32[32,32]{1,0:T(8,128)S(1)}, u32[]{:S(2)}, u32[]{:S(2)}) collective-permute-start(f32[32,32]{1,0:T(8,128)S(1)} %get-tuple-element.617), channel_id=1, source_target_pairs={{0,2},{1,3},{4,6},{5,7},{8,10},{9,11},{12,14},{13,15},{16,18},{17,... | collective-permute-start | bytes 12296 | tf_op jit(solution)/shard_map/ppermute | solution.py:23
  165.9 5.6 %collective-permute-start.1 = (f32[32,32]{1,0:T(8,128)S(1)}, f32[32,32]{1,0:T(8,128)S(1)}, u32[]{:S(2)}, u32[]{:S(2)}) collective-permute-start(f32[32,32]{1,0:T(8,128)S(1)} %get-tuple-element.618), channel_id=1, source_target_pairs={{2,0},{3,1},{6,4},{7,5},{10,8},{11,9},{14,12},{15,13},{18,16},{19,... | collective-permute-start | bytes 12296 | tf_op jit(solution)/shard_map/ppermute | solution.py:26
Sparse Core Ops, SparseCore 0:
  41.8 20.4 reduce-scatter.3
  103.6 53.3 all-reduce.2
where the time goes:
time: 179 us
  waiting for transfers between devices  72.2 us (40%)
  matrix products  39.2 us (22%)
  blocking collectives  35.3 us (20%)
  between operations  14.4 us (8%)
  other arithmetic  6.82 us (4%)
  starting transfers between devices  4.74 us (3%)
  local copies, waits for them, and re-layouts  4.13 us (2%)
  loops' own time  2.33 us (1%)
    psum x1, waiting for transfers between devices, shards(): grad_real, grad_imag = lax.psum((grad_real, grad_imag), ('src', 'row'))  47.8 us
    reduce_scatter x1, waiting for transfers between devices, shards(): lax.psum_scatter(jnp.sum(weights[:, None, None] * (part_real * part_real...  20.5 us
    dot_general x24, matrix products, matmul(): lax.dot_general(left_op, right_op, (((1,), (0,)), ((), ())), precision=la...  18.9 us
    all_gather x1, blocking collectives, shards(): shard_rows = lax.all_gather(window, ('src', 'row'), axis=0, tiled=True)  16.1 us
    all_gather x1, blocking collectives, shards(): cotangent_all = lax.all_gather(cotangent, 'src', axis=0, tiled=True)  13.5 us
    dot_general x14, matrix products, matmul_nt(): lax.dot_general(left_op, right_op, (((1,), (1,)), ((), ())), precision=la...  12 us
    dot_general x14, matrix products, matmul_tn(): lax.dot_general(left_op, right_op, (((0,), (0,)), ((), ())), precision=la...  8.24 us
    psum x1, blocking collectives, shards(): source_sum = lax.psum(source_terms, ('tile', 'row'))  5.67 us
  transfers between devices with their start and end apart: 4, of which 3 were waited for; matrix products, arithmetic and copies ran while one was open for 0% of the time, Pallas kernels for 0%

commit v1 on v0

--- a/solution.py
+++ b/solution.py
@@ -1,8 +1,12 @@
+import functools
 import math
 
 import jax
 import jax.numpy as jnp
+import numpy as np
 from jax import lax
+from jax.experimental import pallas as pl
+from jax.experimental.pallas import tpu as pltpu
 from jax.sharding import PartitionSpec as P
 
 M = 256
@@ -65,7 +69,7 @@
     return (jnp.cos(angles), jnp.sin(angles))
 
 
-def shards(mask_windows, target_windows, pupil_bands, pupil_phase, source_weight):
+def shards_plain(mask_windows, target_windows, pupil_bands, pupil_phase, source_weight):
     src_count = lax.axis_size("src")
     tile_count = lax.axis_size("tile")
     row_count = lax.axis_size("row")
@@ -160,6 +164,410 @@
     return (grad_block[None], source_grad)
 
 
+MESH = pl.DeviceIdType.MESH
+
+
+def pair(values):
+    high = values.astype(jnp.bfloat16)
+    return high, (values - high.astype(jnp.float32)).astype(jnp.bfloat16)
+
+
+def dot_pair(left_op, right_op, contract_right=0):
+    dims = (((1,), (contract_right,)), ((), ()))
+
+    def one(a, b):
+        return lax.dot_general(a, b, dims, preferred_element_type=jnp.float32)
+
+    (left_high, left_low), (right_high, right_low) = left_op, right_op
+    return one(left_high, right_high) + (
+        one(left_high, right_low) + one(left_low, right_high)
+    )
+
+
+def wave_constants(pixels, freqs, src_count, row_count, local_x):
+    freq_index = np.arange(freqs) - freqs // 2
+    angles = 2.0 * np.pi / pixels * (np.outer(freq_index, np.arange(pixels)) % pixels)
+    cos_tab, sin_tab = np.cos(angles), np.sin(angles)
+    wave_y = np.block([[cos_tab, sin_tab], [-sin_tab, cos_tab]])
+    sets = []
+    for row in range(row_count):
+        starts = (np.arange(src_count) * row_count + row) * local_x
+        rows = (starts[:, None] + np.arange(local_x)[None, :]).reshape(-1)
+        c, s = cos_tab[:, rows], sin_tab[:, rows]
+        sets.append(np.block([[c, s], [-s, c]]))
+    wave_x = np.stack(sets)
+    return wave_y, wave_x, np.ascontiguousarray(wave_x.transpose(0, 2, 1))
+
+
+def split_constant(values):
+    values = values.astype(np.float32)
+    high = values.astype(jnp.bfloat16)
+    low = (values - high.astype(np.float32)).astype(jnp.bfloat16)
+    return np.stack([high, low])
+
+
+def kernel(
+    src_count,
+    row_count,
+    tile_count,
+    wy_ref,
+    wx_ref,
+    wxt_ref,
+    mask_ref,
+    goal_ref,
+    band_ref,
+    phase_ref,
+    weight_ref,
+    out_ref,
+    terms_ref,
+    pbuf,
+    tbuf,
+    fbuf,
+    ubuf,
+    part_send,
+    part_recv,
+    cbuf,
+    core_send,
+    core_recv,
+    grad_send,
+    grad_recv,
+    halo_send,
+    halo_recv,
+    term_send,
+    term_recv,
+    mask_ss,
+    mask_rs,
+    fwd_ss,
+    fwd_rs,
+    part_ss,
+    part_rs,
+    cot_ss,
+    cot_rs,
+    core_ss,
+    core_rs,
+    grad_ss,
+    grad_rs,
+    halo_ss,
+    halo_rs,
+    term_ss,
+    term_rs,
+):
+    part = lax.axis_index("parts")
+    src = lax.axis_index("src")
+    tile = lax.axis_index("tile")
+    row = lax.axis_index("row")
+    local_x, pixels = mask_ref.shape[1:]
+    per_device, freqs = phase_ref.shape[:2]
+    sources = per_device * src_count
+    field_scale = 1.0 / (pixels * freqs)
+    other_row = 1 - row
+    other_tile = 1 - tile
+    steps = list(range(1, src_count))
+
+    def ahead(step):
+        return lax.rem(src + step, src_count)
+
+    def behind(step):
+        return lax.rem(src + src_count - step, src_count)
+
+    def to(src_ref, dst_ref, ss, rs, src_at=src, tile_at=tile, row_at=row):
+        return pltpu.make_async_remote_copy(
+            src_ref=src_ref,
+            dst_ref=dst_ref,
+            send_sem=ss,
+            recv_sem=rs,
+            device_id=(part, src_at, tile_at, row_at),
+            device_id_type=MESH,
+        )
+
+    barrier = pltpu.get_barrier_semaphore()
+    near = [(src, tile, other_row), (src, other_tile, row), (src, other_tile, other_row)]
+    peers = [(ahead(step), tile, row) for step in steps] + near
+    for src_at, tile_at, row_at in peers:
+        pl.semaphore_signal(
+            barrier, inc=1, device_id=(part, src_at, tile_at, row_at), device_id_type=MESH
+        )
+
+    wy = (wy_ref[0], wy_ref[1])
+    wf = (wy_ref[0, :, :pixels], wy_ref[1, :, :pixels])
+    own_slot = src * row_count + row
+    pbuf[own_slot] = dot_pair(pair(mask_ref[0]), wf, 1)
+    pl.semaphore_wait(barrier, len(peers))
+
+    own_block = pbuf.at[own_slot]
+    copies = []
+    for step in steps:
+        copy = to(own_block, own_block, mask_ss.at[step], mask_rs.at[step], src_at=ahead(step))
+        copy.start()
+        copies.append(copy)
+    copy = to(own_block, own_block, fwd_ss.at[0], fwd_rs.at[0], row_at=other_row)
+    copy.start()
+    copies.append(copy)
+
+    freq_rows = lax.broadcasted_iota(jnp.int32, (freqs, freqs), 0)
+    pupils = []
+    for one in range(per_device):
+        inside = (freq_rows >= band_ref[one, 0:1, :]) & (freq_rows < band_ref[one, 1:2, :])
+        passing = jnp.where(inside, 1.0, 0.0).T
+        phase = phase_ref[one]
+        pupils.append((passing * jnp.cos(phase), passing * jnp.sin(phase)))
+
+    for step in steps:
+        block = pbuf.at[behind(step) * row_count + row]
+        to(block, block, mask_ss.at[step], mask_rs.at[step], src_at=ahead(step)).wait_recv()
+        copy = to(block, block, fwd_ss.at[step], fwd_rs.at[step], row_at=other_row)
+        copy.start()
+        copies.append(copy)
+    for step in range(src_count):
+        block = pbuf.at[behind(step) * row_count + other_row]
+        to(block, block, fwd_ss.at[step], fwd_rs.at[step], row_at=other_row).wait_recv()
+
+    columns = pair(pbuf[...].reshape(pixels, pixels))
+    spectrum = dot_pair(wf, columns)
+    spec_real = spectrum[:freqs, :freqs] - spectrum[freqs:, freqs:]
+    spec_imag = spectrum[:freqs, freqs:] + spectrum[freqs:, :freqs]
+
+    amps = jnp.concatenate(
+        [
+            jnp.concatenate([pr * spec_real - pi * spec_imag for pr, pi in pupils], axis=1),
+            jnp.concatenate([pi * spec_real + pr * spec_imag for pr, pi in pupils], axis=1),
+        ],
+        axis=0,
+    )
+    wxt = (wxt_ref[0, row], wxt_ref[1, row])
+    swept = dot_pair(wxt, pair(amps)) * field_scale
+    tbuf[...] = swept.reshape(2 * src_count, local_x, per_device * freqs)
+
+    weights = [weight_ref[one] / sources for one in range(per_device)]
+    for step in steps + [0]:
+        block = ahead(step)
+        real, imag = tbuf[block], tbuf[src_count + block]
+        rows = jnp.concatenate(
+            [
+                jnp.concatenate(
+                    [
+                        real[:, one * freqs : (one + 1) * freqs],
+                        imag[:, one * freqs : (one + 1) * freqs],
+                    ],
+                    axis=1,
+                )
+                for one in range(per_device)
+            ],
+            axis=0,
+        )
+        field = dot_pair(pair(rows), wy)
+        fbuf[block] = field
+        squares = field[:, :pixels] * field[:, :pixels] + field[:, pixels:] * field[:, pixels:]
+        total = weights[0] * squares[:local_x]
+        for one in range(1, per_device):
+            total = total + weights[one] * squares[one * local_x : (one + 1) * local_x]
+        part_send[step] = total
+        if step > 0:
+            copy = to(
+                part_send.at[step],
+                part_recv.at[step],
+                part_ss.at[step],
+                part_rs.at[step],
+                src_at=block,
+            )
+            copy.start()
+            copies.append(copy)
+
+    intensity = part_send[0]
+    for step in steps:
+        to(
+            part_send.at[step],
+            part_recv.at[step],
+            part_ss.at[step],
+            part_rs.at[step],
+            src_at=ahead(step),
+        ).wait_recv()
+        intensity = intensity + part_recv[step]
+
+    resist = 1.0 / (1.0 + jnp.exp(-STEEPNESS * (intensity - THRESHOLD)))
+    cotangent = LOSS_SCALE * (resist - goal_ref[0]) * STEEPNESS * resist * (1.0 - resist)
+    cbuf[src] = cotangent
+    for step in steps:
+        block = cbuf.at[src]
+        copy = to(block, block, cot_ss.at[step], cot_rs.at[step], src_at=ahead(step))
+        copy.start()
+        copies.append(copy)
+
+    terms = [jnp.zeros((1, pixels), jnp.float32)] * per_device
+    for step in [0] + steps:
+        block = behind(step)
+        if step > 0:
+            slot = cbuf.at[block]
+            to(slot, slot, cot_ss.at[step], cot_rs.at[step], src_at=ahead(step)).wait_recv()
+        light = cbuf[block]
+        backs = []
+        for one in range(per_device):
+            real = fbuf[block, one * local_x : (one + 1) * local_x, :pixels]
+            imag = fbuf[block, one * local_x : (one + 1) * local_x, pixels:]
+            lit_real, lit_imag = light * real, light * imag
+            scale = 2.0 * weights[one]
+            backs.append(jnp.concatenate([scale * lit_real, scale * lit_imag], axis=1))
+            terms[one] = terms[one] + jnp.sum(
+                lit_real * real + lit_imag * imag, axis=0, keepdims=True
+            )
+        adjoint = dot_pair(pair(jnp.concatenate(backs, axis=0)), wy, 1)
+        for one in range(per_device):
+            rows = slice(one * local_x, (one + 1) * local_x)
+            cols = slice(one * freqs, (one + 1) * freqs)
+            ubuf[block, :, cols] = adjoint[rows, :freqs]
+            ubuf[src_count + block, :, cols] = adjoint[rows, freqs:]
+
+    term_send[...] = jnp.zeros(term_send.shape, jnp.float32)
+    for one in range(per_device):
+        term_send[one : one + 1, :] = terms[one][:, :freqs] + terms[one][:, freqs:]
+    for index, (src_at, tile_at, row_at) in enumerate(near):
+        copy = to(
+            term_send,
+            term_recv.at[index],
+            term_ss.at[index],
+            term_rs.at[index],
+            tile_at=tile_at,
+            row_at=row_at,
+        )
+        copy.start()
+        copies.append(copy)
+
+    wx = (wx_ref[0, row], wx_ref[1, row])
+    swept = ubuf[...].reshape(2 * src_count * local_x, per_device * freqs)
+    swept = dot_pair(wx, pair(swept)) * field_scale
+    grad_real = jnp.zeros((freqs, freqs), jnp.float32)
+    grad_imag = grad_real
+    for one, (pr, pi) in enumerate(pupils):
+        cols = slice(one * freqs, (one + 1) * freqs)
+        real, imag = swept[:freqs, cols], swept[freqs:, cols]
+        grad_real = grad_real + pr * real + pi * imag
+        grad_imag = grad_imag + pr * imag - pi * real
+    grads = pair(jnp.concatenate([grad_real, grad_imag], axis=0))
+
+    def rows_of(index):
+        swept = dot_pair((wxt_ref[0, index], wxt_ref[1, index]), grads)
+        half = src_count * local_x
+        swept = jnp.concatenate([swept[:half], swept[half:]], axis=1)
+        return swept.reshape(src_count, local_x, 2 * freqs)
+
+    core_send[...] = rows_of(other_row)
+    core_copy = to(core_send, core_recv, core_ss, core_rs, row_at=other_row)
+    core_copy.start()
+    copies.append(core_copy)
+    grad_send[...] = rows_of(row)
+    core_copy.wait_recv()
+    for step in steps:
+        block = ahead(step)
+        grad_send[block] = grad_send[block] + core_recv[block]
+        copy = to(
+            grad_send.at[block],
+            grad_recv.at[step],
+            grad_ss.at[step],
+            grad_rs.at[step],
+            src_at=block,
+        )
+        copy.start()
+        copies.append(copy)
+    total = grad_send[src] + core_recv[src]
+    for step in steps:
+        to(
+            grad_send.at[ahead(step)],
+            grad_recv.at[step],
+            grad_ss.at[step],
+            grad_rs.at[step],
+            src_at=ahead(step),
+        ).wait_recv()
+        total = total + grad_recv[step]
+    grad_block = dot_pair(pair(total), wf)
+
+    low, high = grad_block[:, :freqs], grad_block[:, pixels - freqs :]
+    halo_send[...] = jnp.where(tile == 0, high, low)
+    halo_copy = to(halo_send, halo_recv, halo_ss, halo_rs, tile_at=other_tile)
+    halo_copy.start()
+    copies.append(halo_copy)
+
+    for index, (src_at, tile_at, row_at) in enumerate(near):
+        to(
+            term_send,
+            term_recv.at[index],
+            term_ss.at[index],
+            term_rs.at[index],
+            tile_at=tile_at,
+            row_at=row_at,
+        ).wait_recv()
+    total = (term_send[...] + term_recv[0]) + (term_recv[1] + term_recv[2])
+    total = total / (sources * pixels * tile_count)
+    for one in range(per_device):
+        terms_ref[one] = jnp.sum(total[one : one + 1, :])
+
+    halo_copy.wait_recv()
+    lanes = lax.broadcasted_iota(jnp.int32, (local_x, freqs), 1)
+    strip = halo_recv[...]
+    from_below = jnp.where(
+        (lanes < OV) & (tile == 1), pltpu.roll(strip, OV, axis=1), 0.0
+    )
+    from_above = jnp.where(
+        (lanes >= freqs - OV) & (tile == 0), pltpu.roll(strip, freqs - OV, axis=1), 0.0
+    )
+    out_ref[0, :, :freqs] = low + from_below
+    out_ref[0, :, pixels - freqs :] = high + from_above
+    for copy in copies:
+        copy.wait_send()
+
+
+def shards(mask_windows, target_windows, pupil_bands, pupil_phase, source_weight):
+    src_count = lax.axis_size("src")
+    tile_count = lax.axis_size("tile")
+    row_count = lax.axis_size("row")
+    local_x, pixels = mask_windows.shape[1:]
+    per_device, freqs = pupil_phase.shape[:2]
+    fits = row_count == 2 and tile_count == 2 and src_count > 1
+    if not fits or local_x % 8 != 0 or freqs % 128 != 0 or pixels != 2 * freqs:
+        return shards_plain(
+            mask_windows, target_windows, pupil_bands, pupil_phase, source_weight
+        )
+    tables = [
+        split_constant(one)
+        for one in wave_constants(pixels, freqs, src_count, row_count, local_x)
+    ]
+    bands = jnp.transpose(pupil_bands, (0, 2, 1))
+    in_vmem = pl.BlockSpec(memory_space=pltpu.VMEM)
+    in_smem = pl.BlockSpec(memory_space=pltpu.SMEM)
+    f32 = jnp.float32
+    block = (local_x, pixels)
+    dma = pltpu.SemaphoreType.DMA
+    return pl.pallas_call(
+        functools.partial(kernel, src_count, row_count, tile_count),
+        out_shape=(
+            jax.ShapeDtypeStruct(mask_windows.shape, f32),
+            jax.ShapeDtypeStruct(source_weight.shape, f32),
+        ),
+        in_specs=[in_vmem] * 7 + [in_smem],
+        out_specs=(in_vmem, in_smem),
+        scratch_shapes=[
+            pltpu.VMEM((src_count * row_count,) + block, f32),
+            pltpu.VMEM((2 * src_count, local_x, per_device * freqs), f32),
+            pltpu.VMEM((src_count, per_device * local_x, 2 * pixels), f32),
+            pltpu.VMEM((2 * src_count, local_x, per_device * freqs), f32),
+        ]
+        + [pltpu.VMEM((src_count,) + block, f32)] * 7
+        + [
+            pltpu.VMEM((local_x, freqs), f32),
+            pltpu.VMEM((local_x, freqs), f32),
+            pltpu.VMEM((8, freqs), f32),
+            pltpu.VMEM((3, 8, freqs), f32),
+        ]
+        + [dma((src_count,))] * 8
+        + [dma(()), dma(())]
+        + [dma((src_count,))] * 2
+        + [dma(()), dma(())]
+        + [dma((3,))] * 2,
+        compiler_params=pltpu.CompilerParams(
+            collective_id=0, has_side_effects=True, vmem_limit_bytes=48 * 1024 * 1024
+        ),
+    )(*tables, mask_windows, target_windows, bands, pupil_phase, source_weight)
+
+
 def solution(mesh):
     return jax.shard_map(
         shards,

time: 179 us -> 41.5 us (0.23)
  waiting for transfers between devices: 72.2 us -> 0 us
  matrix products: 39.2 us -> 0 us
  blocking collectives: 35.3 us -> 0 us
  Pallas kernels: 0 us -> 32.4 us
  between operations: 14.4 us -> 0.66 us
  other arithmetic: 6.82 us -> 0 us
  starting transfers between devices: 4.74 us -> 0 us
  local copies, waits for them, and re-layouts: 4.13 us -> 8.02 us
  loops' own time: 2.33 us -> 0 us
    psum x1 -> x0, waiting for transfers between devices: 47.8 us -> none  [shards(): grad_real, grad_imag = lax.psum((grad_real, grad_imag), ('src', 'row'))]
    dot_general x52 -> x0, matrix products: 39.2 us -> none  [the longest x24 18.9 us: matmul(): lax.dot_general(left_op, right_op, (((1,), (0,)), ((), ())), precision=la...]
    pallas_call x0 -> x1, Pallas kernels: none -> 32.4 us  [shards(): pl.pallas_call(functools.partial(kernel, src_count, row_count, tile_count...]
    all_gather x2 -> x0, blocking collectives: 29.7 us -> none  [the longest x1 16.1 us: shards(): shard_rows = lax.all_gather(window, ('src', 'row'), axis=0, tiled=True)]
    reduce_scatter x1 -> x0, waiting for transfers between devices: 20.5 us -> none  [shards(): lax.psum_scatter(jnp.sum(weights[:, None, None] * (part_real * part_real...]
    unnamed x18, local copies, waits for them, and re-layouts: 1.48 us -> 8.02 us
    psum x1 -> x0, blocking collectives: 5.67 us -> none  [shards(): source_sum = lax.psum(source_terms, ('tile', 'row'))]
    ppermute x2 -> x0, starting transfers between devices: 4.66 us -> none  [the longest x1 3.37 us: with_halo(): lax.ppermute(lax.slice_in_dim(block, block.shape[dim] - width, None, axis...]
  transfers between devices with their start and end apart: 4 -> 0, of which waited for: 3 -> 0; matrix products, arithmetic and copies ran while one was open for 0% -> 0% of each run, Pallas kernels for 0% -> 0%
where the time goes in v1:
time: 41.5 us; the launch traced here: 41.1 us
  Pallas kernels  32.4 us (78%)
  local copies, waits for them, and re-layouts  8.02 us (19%)
  between operations  0.66 us (2%)
    pallas_call x1, Pallas kernels, shards(): pl.pallas_call(functools.partial(kernel, src_count, row_count, tile_count...  32.4 us
    unnamed x18, local copies, waits for them, and re-layouts  8.02 us

profile of v1, /device:TPU:0, one launch (start us, length us, event | category | flops | bytes accessed | tf_op | source)
XLA Modules:
  0.0 41.1 jit_solution(17537363158079934990)
XLA Ops:
  0.6 0.0 copy-start.7
  0.6 0.6 %copy-done.7 = f32[3]{0:T(128)S(1)} copy-done((f32[3]{0:T(128)S(1)}, f32[3]{0:T(128)}, u32[]{:S(2)}) %copy-start.7) | copy-done | bytes 36
  1.3 0.0 copy-start
  1.3 1.0 %copy-done = bf16[2,2,256,256]{3,2,1,0:T(8,128)(2,1)S(1)} copy-done((bf16[2,2,256,256]{3,2,1,0:T(8,128)(2,1)S(1)}, bf16[2,2,256,256]{3,2,1,0:T(8,128)(2,1)}, u32[]{:S(2)}) %copy-start) | copy-done | bytes 524312
  2.3 0.0 copy-start.1
  2.3 1.0 %copy-done.1 = bf16[2,2,256,256]{3,2,1,0:T(8,128)(2,1)S(1)} copy-done((bf16[2,2,256,256]{3,2,1,0:T(8,128)(2,1)S(1)}, bf16[2,2,256,256]{3,2,1,0:T(8,128)(2,1)}, u32[]{:S(2)}) %copy-start.1) | copy-done | bytes 524312
  3.4 0.0 copy-start.2
  3.4 1.0 %copy-done.2 = bf16[2,256,512]{2,1,0:T(8,128)(2,1)S(1)} copy-done((bf16[2,256,512]{2,1,0:T(8,128)(2,1)S(1)}, bf16[2,256,512]{2,1,0:T(8,128)(2,1)}, u32[]{:S(2)}) %copy-start.2) | copy-done | bytes 524312
  4.4 0.0 copy-start.3
  4.4 0.9 %copy-done.3 = f32[3,128,128]{2,1,0:T(8,128)S(1)} copy-done((f32[3,128,128]{2,1,0:T(8,128)S(1)}, f32[3,128,128]{2,1,0:T(8,128)}, u32[]{:S(2)}) %copy-start.3) | copy-done | bytes 196632
  5.3 0.0 copy-start.4
  5.3 0.8 %copy-done.4 = f32[1,32,256]{2,1,0:T(8,128)S(1)} copy-done((f32[1,32,256]{2,1,0:T(8,128)S(1)}, f32[1,32,256]{2,1,0:T(8,128)}, u32[]{:S(2)}) %copy-start.4) | copy-done | bytes 32792
  6.1 0.0 copy-start.5
  6.1 0.8 %copy-done.5 = f32[1,32,256]{2,1,0:T(8,128)S(1)} copy-done((f32[1,32,256]{2,1,0:T(8,128)S(1)}, f32[1,32,256]{2,1,0:T(8,128)}, u32[]{:S(2)}) %copy-start.5) | copy-done | bytes 32792
  6.9 0.0 copy-start.6
  6.9 0.7 %copy-done.6 = s32[3,128,2]{1,2,0:T(2,128)S(1)} copy-done((s32[3,128,2]{1,2,0:T(2,128)S(1)}, s32[3,128,2]{1,2,0:T(2,128)}, u32[]{:S(2)}) %copy-start.6) | copy-done | bytes 3096
  7.5 32.4 %shard_map.95 = (f32[1,32,256]{2,1,0:T(8,128)S(1)}, f32[3]{0:T(128)S(1)}) custom-call(bf16[2,256,512]{2,1,0:T(8,128)(2,1)S(1)} %copy-done.2, bf16[2,2,256,256]{3,2,1,0:T(8,128)(2,1)S(1)} %copy-done.1, bf16[2,2,256,256]{3,2,1,0:T(8,128)(2,1)S(1)} %copy-done, f32[1,32,256]{2,1,0:T(8,128)S(1)} %copy-done.4, f32[1,32,256]{2,1,0:T(8,128)S(1)} %copy-done.5, ...), custom_call_target="tpu_custom_call" | custom-call | tf_op jit(solution)/shard_map/pallas_call | solution.py:539
  39.9 0.6 %copy.12 = f32[1,32,256]{2,1,0:T(8,128)} copy(f32[1,32,256]{2,1,0:T(8,128)S(1)} %get-tuple-element.4) | data formatting | bytes 65536
  40.6 0.5 %copy.13 = f32[3]{0:T(128)} copy(f32[3]{0:T(128)S(1)} %get-tuple-element.5) | data formatting | bytes 24
Async XLA Ops:
  0.6 0.7 %copy-start.7 = (f32[3]{0:T(128)S(1)}, f32[3]{0:T(128)}, u32[]{:S(2)}) copy-start(f32[3]{0:T(128)} %weight_ref.1) | copy-start | bytes 40
  1.3 1.0 %copy-start = (bf16[2,2,256,256]{3,2,1,0:T(8,128)(2,1)S(1)}, bf16[2,2,256,256]{3,2,1,0:T(8,128)(2,1)}, u32[]{:S(2)}) copy-start(bf16[2,2,256,256]{3,2,1,0:T(8,128)(2,1)} %constant.8.clone.wxt_ref) | copy-start | bytes 1572868
  2.3 1.0 %copy-start.1 = (bf16[2,2,256,256]{3,2,1,0:T(8,128)(2,1)S(1)}, bf16[2,2,256,256]{3,2,1,0:T(8,128)(2,1)}, u32[]{:S(2)}) copy-start(bf16[2,2,256,256]{3,2,1,0:T(8,128)(2,1)} %constant.7.clone.wx_ref) | copy-start | bytes 1572868
  3.4 1.0 %copy-start.2 = (bf16[2,256,512]{2,1,0:T(8,128)(2,1)S(1)}, bf16[2,256,512]{2,1,0:T(8,128)(2,1)}, u32[]{:S(2)}) copy-start(bf16[2,256,512]{2,1,0:T(8,128)(2,1)} %constant.6.clone.wy_ref) | copy-start | bytes 1572868
  4.4 0.9 %copy-start.3 = (f32[3,128,128]{2,1,0:T(8,128)S(1)}, f32[3,128,128]{2,1,0:T(8,128)}, u32[]{:S(2)}) copy-start(f32[3,128,128]{2,1,0:T(8,128)} %phase_ref.1) | copy-start | bytes 589828
  5.3 0.8 %copy-start.4 = (f32[1,32,256]{2,1,0:T(8,128)S(1)}, f32[1,32,256]{2,1,0:T(8,128)}, u32[]{:S(2)}) copy-start(f32[1,32,256]{2,1,0:T(8,128)} %mask_ref.1) | copy-start | bytes 98308
  6.1 0.8 %copy-start.5 = (f32[1,32,256]{2,1,0:T(8,128)S(1)}, f32[1,32,256]{2,1,0:T(8,128)}, u32[]{:S(2)}) copy-start(f32[1,32,256]{2,1,0:T(8,128)} %goal_ref.1) | copy-start | bytes 98308
  6.9 0.7 %copy-start.6 = (s32[3,128,2]{1,2,0:T(2,128)S(1)}, s32[3,128,2]{1,2,0:T(2,128)}, u32[]{:S(2)}) copy-start(s32[3,128,2]{1,2,0:T(2,128)} %param.10) | copy-start | bytes 9220

commit v2 on v1

--- a/solution.py
+++ b/solution.py
@@ -210,6 +210,16 @@
     src_count,
     row_count,
     tile_count,
+    wy_hbm,
+    wx_hbm,
+    wxt_hbm,
+    mask_hbm,
+    goal_hbm,
+    band_hbm,
+    phase_hbm,
+    weight_hbm,
+    out_ref,
+    terms_ref,
     wy_ref,
     wx_ref,
     wxt_ref,
@@ -218,8 +228,7 @@
     band_ref,
     phase_ref,
     weight_ref,
-    out_ref,
-    terms_ref,
+    load_sems,
     pbuf,
     tbuf,
     fbuf,
@@ -260,6 +269,21 @@
     per_device, freqs = phase_ref.shape[:2]
     sources = per_device * src_count
     field_scale = 1.0 / (pixels * freqs)
+    loads = {}
+    for index, (name, source, target) in enumerate(
+        [
+            ("mask", mask_hbm, mask_ref),
+            ("wy", wy_hbm, wy_ref),
+            ("phase", phase_hbm, phase_ref),
+            ("band", band_hbm, band_ref),
+            ("wxt", wxt_hbm, wxt_ref),
+            ("weight", weight_hbm, weight_ref),
+            ("goal", goal_hbm, goal_ref),
+            ("wx", wx_hbm.at[:, row], wx_ref),
+        ]
+    ):
+        loads[name] = pltpu.make_async_copy(source, target, load_sems.at[index])
+        loads[name].start()
     other_row = 1 - row
     other_tile = 1 - tile
     steps = list(range(1, src_count))
@@ -288,6 +312,8 @@
             barrier, inc=1, device_id=(part, src_at, tile_at, row_at), device_id_type=MESH
         )
 
+    loads["mask"].wait()
+    loads["wy"].wait()
     wy = (wy_ref[0], wy_ref[1])
     wf = (wy_ref[0, :, :pixels], wy_ref[1, :, :pixels])
     own_slot = src * row_count + row
@@ -304,6 +330,8 @@
     copy.start()
     copies.append(copy)
 
+    loads["phase"].wait()
+    loads["band"].wait()
     freq_rows = lax.broadcasted_iota(jnp.int32, (freqs, freqs), 0)
     pupils = []
     for one in range(per_device):
@@ -312,6 +340,8 @@
         phase = phase_ref[one]
         pupils.append((passing * jnp.cos(phase), passing * jnp.sin(phase)))
 
+    for name in ("wxt", "weight", "goal", "wx"):
+        loads[name].wait()
     for step in steps:
         block = pbuf.at[behind(step) * row_count + row]
         to(block, block, mask_ss.at[step], mask_rs.at[step], src_at=ahead(step)).wait_recv()
@@ -432,7 +462,7 @@
         copy.start()
         copies.append(copy)
 
-    wx = (wx_ref[0, row], wx_ref[1, row])
+    wx = (wx_ref[0], wx_ref[1])
     swept = ubuf[...].reshape(2 * src_count * local_x, per_device * freqs)
     swept = dot_pair(wx, pair(swept)) * field_scale
     grad_real = jnp.zeros((freqs, freqs), jnp.float32)
@@ -542,9 +572,18 @@
             jax.ShapeDtypeStruct(mask_windows.shape, f32),
             jax.ShapeDtypeStruct(source_weight.shape, f32),
         ),
-        in_specs=[in_vmem] * 7 + [in_smem],
+        in_specs=[pl.BlockSpec(memory_space=pltpu.HBM)] * 8,
         out_specs=(in_vmem, in_smem),
         scratch_shapes=[
+            pltpu.VMEM(tables[0].shape, tables[0].dtype),
+            pltpu.VMEM(tables[1].shape[:1] + tables[1].shape[2:], tables[1].dtype),
+            pltpu.VMEM(tables[2].shape, tables[2].dtype),
+            pltpu.VMEM(mask_windows.shape, f32),
+            pltpu.VMEM(target_windows.shape, f32),
+            pltpu.VMEM(bands.shape, bands.dtype),
+            pltpu.VMEM(pupil_phase.shape, f32),
+            pltpu.SMEM(source_weight.shape, f32),
+            dma((8,)),
             pltpu.VMEM((src_count * row_count,) + block, f32),
             pltpu.VMEM((2 * src_count, local_x, per_device * freqs), f32),
             pltpu.VMEM((src_count, per_device * local_x, 2 * pixels), f32),
@@ -563,7 +602,7 @@
         + [dma(()), dma(())]
         + [dma((3,))] * 2,
         compiler_params=pltpu.CompilerParams(
-            collective_id=0, has_side_effects=True, vmem_limit_bytes=48 * 1024 * 1024
+            collective_id=0, has_side_effects=True, vmem_limit_bytes=63 * 1024 * 1024
         ),
     )(*tables, mask_windows, target_windows, bands, pupil_phase, source_weight)
 

time: 41.5 us -> 34.7 us (0.84)
  local copies, waits for them, and re-layouts: 8.02 us -> 1.89 us
    unnamed x18 -> x4, local copies, waits for them, and re-layouts: 8.02 us -> 1.89 us
    pallas_call x1, Pallas kernels: 32.4 us -> 32 us  [shards(): pl.pallas_call(functools.partial(kernel, src_count, row_count, tile_count...]
where the time goes in v2:
time: 34.7 us; the launch traced here: 34.5 us
  Pallas kernels  32 us (92%)
  local copies, waits for them, and re-layouts  1.89 us (5%)
  between operations  0.65 us (2%)
    pallas_call x1, Pallas kernels, shards(): pl.pallas_call(functools.partial(kernel, src_count, row_count, tile_count...  32 us
    unnamed x4, local copies, waits for them, and re-layouts  1.89 us

profile of v2, /device:TPU:0, one launch (start us, length us, event | category | flops | bytes accessed | tf_op | source)
XLA Modules:
  0.0 34.5 jit_solution(16210804952874474289)
XLA Ops:
  0.6 32.0 %shard_map.95 = (f32[1,32,256]{2,1,0:T(8,128)}, f32[3]{0:T(128)}) custom-call(bf16[2,256,512]{2,1,0:T(8,128)(2,1)} %constant.6.clone.wy_hbm, bf16[2,2,256,256]{3,2,1,0:T(8,128)(2,1)} %constant.7.clone.wx_hbm, bf16[2,2,256,256]{3,2,1,0:T(8,128)(2,1)} %constant.8.clone.wxt_hbm, f32[1,32,256]{2,1,0:T(8,128)} %mask_hbm.1, f32[1,32,256]{2,1,0:T(8,128)} %goal_hbm.1, ...), custom_call_target="tpu_custom_call" | custom-call | tf_op jit(solution)/shard_map/pallas_call | solution.py:569
  32.6 0.0 copy-start
  32.6 1.4 %copy.12 = f32[1,32,256]{2,1,0:T(8,128)} copy(f32[1,32,256]{2,1,0:T(8,128)} %get-tuple-element.4) | data formatting | bytes 65536
  34.0 0.0 copy-done
  34.0 0.5 %copy.13 = f32[3]{0:T(128)} copy(f32[3]{0:T(128)S(1)} %copy-done) | data formatting | bytes 24
Async XLA Ops:
  32.6 1.4 %copy-start = (f32[3]{0:T(128)S(1)}, f32[3]{0:T(128)}, u32[]{:S(2)}) copy-start(f32[3]{0:T(128)} %get-tuple-element.5) | copy-start | bytes 40

commit v3 on v2

--- a/solution.py
+++ b/solution.py
@@ -286,13 +286,15 @@
         loads[name].start()
     other_row = 1 - row
     other_tile = 1 - tile
-    steps = list(range(1, src_count))
-
-    def ahead(step):
-        return lax.rem(src + step, src_count)
-
-    def behind(step):
-        return lax.rem(src + src_count - step, src_count)
+    last = src_count - 1
+
+    def far(step):
+        up = last - src
+        side = lax.div(up + last - step, src_count)
+        return side * (last - step) + (1 - side) * (step - up)
+
+    far_first = [far(step) for step in range(last)]
+    near_first = far_first[::-1]
 
     def to(src_ref, dst_ref, ss, rs, src_at=src, tile_at=tile, row_at=row):
         return pltpu.make_async_remote_copy(
@@ -306,7 +308,7 @@
 
     barrier = pltpu.get_barrier_semaphore()
     near = [(src, tile, other_row), (src, other_tile, row), (src, other_tile, other_row)]
-    peers = [(ahead(step), tile, row) for step in steps] + near
+    peers = [(peer, at, row) for peer in far_first for at in (tile, other_tile)] + near
     for src_at, tile_at, row_at in peers:
         pl.semaphore_signal(
             barrier, inc=1, device_id=(part, src_at, tile_at, row_at), device_id_type=MESH
@@ -322,11 +324,11 @@
 
     own_block = pbuf.at[own_slot]
     copies = []
-    for step in steps:
-        copy = to(own_block, own_block, mask_ss.at[step], mask_rs.at[step], src_at=ahead(step))
+    for peer in far_first:
+        copy = to(own_block, own_block, mask_ss.at[peer], mask_rs.at[src], src_at=peer)
         copy.start()
         copies.append(copy)
-    copy = to(own_block, own_block, fwd_ss.at[0], fwd_rs.at[0], row_at=other_row)
+    copy = to(own_block, own_block, fwd_ss.at[src], fwd_rs.at[src], row_at=other_row)
     copy.start()
     copies.append(copy)
 
@@ -342,15 +344,15 @@
 
     for name in ("wxt", "weight", "goal", "wx"):
         loads[name].wait()
-    for step in steps:
-        block = pbuf.at[behind(step) * row_count + row]
-        to(block, block, mask_ss.at[step], mask_rs.at[step], src_at=ahead(step)).wait_recv()
-        copy = to(block, block, fwd_ss.at[step], fwd_rs.at[step], row_at=other_row)
+    for peer in near_first:
+        block = pbuf.at[peer * row_count + row]
+        to(block, block, mask_ss.at[peer], mask_rs.at[peer], src_at=peer).wait_recv()
+        copy = to(block, block, fwd_ss.at[peer], fwd_rs.at[peer], row_at=other_row)
         copy.start()
         copies.append(copy)
-    for step in range(src_count):
-        block = pbuf.at[behind(step) * row_count + other_row]
-        to(block, block, fwd_ss.at[step], fwd_rs.at[step], row_at=other_row).wait_recv()
+    for peer in [src] + near_first:
+        block = pbuf.at[peer * row_count + other_row]
+        to(block, block, fwd_ss.at[peer], fwd_rs.at[peer], row_at=other_row).wait_recv()
 
     columns = pair(pbuf[...].reshape(pixels, pixels))
     spectrum = dot_pair(wf, columns)
@@ -369,8 +371,7 @@
     tbuf[...] = swept.reshape(2 * src_count, local_x, per_device * freqs)
 
     weights = [weight_ref[one] / sources for one in range(per_device)]
-    for step in steps + [0]:
-        block = ahead(step)
+    for block in far_first + [src]:
         real, imag = tbuf[block], tbuf[src_count + block]
         rows = jnp.concatenate(
             [
@@ -391,44 +392,43 @@
         total = weights[0] * squares[:local_x]
         for one in range(1, per_device):
             total = total + weights[one] * squares[one * local_x : (one + 1) * local_x]
-        part_send[step] = total
-        if step > 0:
+        if block is not src:
+            part_send[block] = total
             copy = to(
-                part_send.at[step],
-                part_recv.at[step],
-                part_ss.at[step],
-                part_rs.at[step],
+                part_send.at[block],
+                part_recv.at[src],
+                part_ss.at[block],
+                part_rs.at[src],
                 src_at=block,
             )
             copy.start()
             copies.append(copy)
 
-    intensity = part_send[0]
-    for step in steps:
+    intensity = total
+    for peer in near_first:
         to(
-            part_send.at[step],
-            part_recv.at[step],
-            part_ss.at[step],
-            part_rs.at[step],
-            src_at=ahead(step),
+            part_send.at[peer],
+            part_recv.at[peer],
+            part_ss.at[peer],
+            part_rs.at[peer],
+            src_at=peer,
         ).wait_recv()
-        intensity = intensity + part_recv[step]
+        intensity = intensity + part_recv[peer]
 
     resist = 1.0 / (1.0 + jnp.exp(-STEEPNESS * (intensity - THRESHOLD)))
     cotangent = LOSS_SCALE * (resist - goal_ref[0]) * STEEPNESS * resist * (1.0 - resist)
     cbuf[src] = cotangent
-    for step in steps:
+    for peer in far_first:
         block = cbuf.at[src]
-        copy = to(block, block, cot_ss.at[step], cot_rs.at[step], src_at=ahead(step))
+        copy = to(block, block, cot_ss.at[peer], cot_rs.at[src], src_at=peer)
         copy.start()
         copies.append(copy)
 
     terms = [jnp.zeros((1, pixels), jnp.float32)] * per_device
-    for step in [0] + steps:
-        block = behind(step)
-        if step > 0:
+    for block in [src] + near_first:
+        if block is not src:
             slot = cbuf.at[block]
-            to(slot, slot, cot_ss.at[step], cot_rs.at[step], src_at=ahead(step)).wait_recv()
+            to(slot, slot, cot_ss.at[block], cot_rs.at[block], src_at=block).wait_recv()
         light = cbuf[block]
         backs = []
         for one in range(per_device):
@@ -486,35 +486,52 @@
     copies.append(core_copy)
     grad_send[...] = rows_of(row)
     core_copy.wait_recv()
-    for step in steps:
-        block = ahead(step)
-        grad_send[block] = grad_send[block] + core_recv[block]
+    for peer in far_first:
+        grad_send[peer] = grad_send[peer] + core_recv[peer]
         copy = to(
-            grad_send.at[block],
-            grad_recv.at[step],
-            grad_ss.at[step],
-            grad_rs.at[step],
-            src_at=block,
+            grad_send.at[peer],
+            grad_recv.at[src],
+            grad_ss.at[peer],
+            grad_rs.at[src],
+            src_at=peer,
         )
         copy.start()
         copies.append(copy)
-    total = grad_send[src] + core_recv[src]
-    for step in steps:
-        to(
-            grad_send.at[ahead(step)],
-            grad_recv.at[step],
-            grad_ss.at[step],
-            grad_rs.at[step],
-            src_at=ahead(step),
-        ).wait_recv()
-        total = total + grad_recv[step]
-    grad_block = dot_pair(pair(total), wf)
-
-    low, high = grad_block[:, :freqs], grad_block[:, pixels - freqs :]
-    halo_send[...] = jnp.where(tile == 0, high, low)
-    halo_copy = to(halo_send, halo_recv, halo_ss, halo_rs, tile_at=other_tile)
-    halo_copy.start()
-    copies.append(halo_copy)
+    grad_send[src] = grad_send[src] + core_recv[src]
+
+    lanes = lax.broadcasted_iota(jnp.int32, (local_x, freqs), 1)
+    edge_wave = tuple(
+        jnp.where(
+            tile == 0,
+            wy_ref[index, :, pixels - freqs : pixels].astype(jnp.float32),
+            wy_ref[index, :, :freqs].astype(jnp.float32),
+        ).astype(jnp.bfloat16)
+        for index in range(2)
+    )
+    edges = grad_send[...].reshape(src_count * local_x, 2 * freqs)
+    edges = dot_pair(pair(edges), edge_wave).reshape(src_count, local_x, freqs)
+    fold = freqs // OV
+    depth = local_x // fold
+    for block in range(src_count):
+        strip = jnp.where(tile == 0, pltpu.roll(edges[block], OV, axis=1), edges[block])
+        strip = jnp.where(lanes < OV, strip, 0.0)
+        packed = strip[:depth]
+        for one in range(1, fold):
+            packed = packed + pltpu.roll(
+                strip[one * depth : (one + 1) * depth], one * OV, axis=1
+            )
+        halo_send[block] = packed
+    for peer in far_first + [src]:
+        copy = to(
+            halo_send.at[peer],
+            halo_recv.at[src],
+            halo_ss.at[peer],
+            halo_rs.at[src],
+            src_at=peer,
+            tile_at=other_tile,
+        )
+        copy.start()
+        copies.append(copy)
 
     for index, (src_at, tile_at, row_at) in enumerate(near):
         to(
@@ -530,12 +547,36 @@
     for one in range(per_device):
         terms_ref[one] = jnp.sum(total[one : one + 1, :])
 
-    halo_copy.wait_recv()
-    lanes = lax.broadcasted_iota(jnp.int32, (local_x, freqs), 1)
-    strip = halo_recv[...]
-    from_below = jnp.where(
-        (lanes < OV) & (tile == 1), pltpu.roll(strip, OV, axis=1), 0.0
-    )
+    total = grad_send[src]
+    for peer in near_first:
+        to(
+            grad_send.at[peer],
+            grad_recv.at[peer],
+            grad_ss.at[peer],
+            grad_rs.at[peer],
+            src_at=peer,
+        ).wait_recv()
+        total = total + grad_recv[peer]
+    grad_block = dot_pair(pair(total), wf)
+    low, high = grad_block[:, :freqs], grad_block[:, pixels - freqs :]
+
+    packed = jnp.zeros((depth, freqs), jnp.float32)
+    for peer in [src] + near_first:
+        to(
+            halo_send.at[peer],
+            halo_recv.at[peer],
+            halo_ss.at[peer],
+            halo_rs.at[peer],
+            src_at=peer,
+            tile_at=other_tile,
+        ).wait_recv()
+        packed = packed + halo_recv[peer]
+    strip = jnp.concatenate(
+        [packed]
+        + [pltpu.roll(packed, freqs - one * OV, axis=1) for one in range(1, fold)],
+        axis=0,
+    )
+    from_below = jnp.where((lanes < OV) & (tile == 1), strip, 0.0)
     from_above = jnp.where(
         (lanes >= freqs - OV) & (tile == 0), pltpu.roll(strip, freqs - OV, axis=1), 0.0
     )
@@ -552,7 +593,7 @@
     local_x, pixels = mask_windows.shape[1:]
     per_device, freqs = pupil_phase.shape[:2]
     fits = row_count == 2 and tile_count == 2 and src_count > 1
-    if not fits or local_x % 8 != 0 or freqs % 128 != 0 or pixels != 2 * freqs:
+    if not fits or local_x % 32 != 0 or freqs % 128 != 0 or pixels != 2 * freqs or OV != 32:
         return shards_plain(
             mask_windows, target_windows, pupil_bands, pupil_phase, source_weight
         )
@@ -591,15 +632,14 @@
         ]
         + [pltpu.VMEM((src_count,) + block, f32)] * 7
         + [
-            pltpu.VMEM((local_x, freqs), f32),
-            pltpu.VMEM((local_x, freqs), f32),
+            pltpu.VMEM((src_count, local_x * OV // freqs, freqs), f32),
+            pltpu.VMEM((src_count, local_x * OV // freqs, freqs), f32),
             pltpu.VMEM((8, freqs), f32),
             pltpu.VMEM((3, 8, freqs), f32),
         ]
         + [dma((src_count,))] * 8
         + [dma(()), dma(())]
-        + [dma((src_count,))] * 2
-        + [dma(()), dma(())]
+        + [dma((src_count,))] * 4
         + [dma((3,))] * 2,
         compiler_params=pltpu.CompilerParams(
             collective_id=0, has_side_effects=True, vmem_limit_bytes=63 * 1024 * 1024

time: 34.7 us -> 34 us (0.980)
  Pallas kernels: 32 us -> 31.3 us
    pallas_call x1, Pallas kernels: 32 us -> 31.3 us  [shards(): pl.pallas_call(functools.partial(kernel, src_count, row_count, tile_count...]
where the time goes in v3:
time: 34 us; the launch traced here: 33.8 us
  Pallas kernels  31.3 us (92%)
  local copies, waits for them, and re-layouts  1.89 us (6%)
  between operations  0.65 us (2%)
    pallas_call x1, Pallas kernels, shards(): pl.pallas_call(functools.partial(kernel, src_count, row_count, tile_count...  31.3 us
    unnamed x4, local copies, waits for them, and re-layouts  1.89 us

profile of v3, /device:TPU:0, one launch (start us, length us, event | category | flops | bytes accessed | tf_op | source)
XLA Modules:
  0.0 33.8 jit_solution(3023390835221714056)
XLA Ops:
  0.6 31.3 %shard_map.95 = (f32[1,32,256]{2,1,0:T(8,128)}, f32[3]{0:T(128)}) custom-call(bf16[2,256,512]{2,1,0:T(8,128)(2,1)} %constant.6.clone.wy_hbm, bf16[2,2,256,256]{3,2,1,0:T(8,128)(2,1)} %constant.7.clone.wx_hbm, bf16[2,2,256,256]{3,2,1,0:T(8,128)(2,1)} %constant.8.clone.wxt_hbm, f32[1,32,256]{2,1,0:T(8,128)} %mask_hbm.1, f32[1,32,256]{2,1,0:T(8,128)} %goal_hbm.1, ...), custom_call_target="tpu_custom_call" | custom-call | tf_op jit(solution)/shard_map/pallas_call | solution.py:610
  31.9 0.0 copy-start
  31.9 1.4 %copy.12 = f32[1,32,256]{2,1,0:T(8,128)} copy(f32[1,32,256]{2,1,0:T(8,128)} %get-tuple-element.4) | data formatting | bytes 65536
  33.3 0.0 copy-done
  33.3 0.5 %copy.13 = f32[3]{0:T(128)} copy(f32[3]{0:T(128)S(1)} %copy-done) | data formatting | bytes 24
Async XLA Ops:
  31.9 1.4 %copy-start = (f32[3]{0:T(128)S(1)}, f32[3]{0:T(128)}, u32[]{:S(2)}) copy-start(f32[3]{0:T(128)} %get-tuple-element.5) | copy-start | bytes 40

commit v4 on v3

--- a/solution.py
+++ b/solution.py
@@ -308,7 +308,7 @@
 
     barrier = pltpu.get_barrier_semaphore()
     near = [(src, tile, other_row), (src, other_tile, row), (src, other_tile, other_row)]
-    peers = [(peer, at, row) for peer in far_first for at in (tile, other_tile)] + near
+    peers = [(peer, tile, row) for peer in far_first] + near
     for src_at, tile_at, row_at in peers:
         pl.semaphore_signal(
             barrier, inc=1, device_id=(part, src_at, tile_at, row_at), device_id_type=MESH

time: 34 us -> 34 us (level)
  no operation moved by 1% of the time
where the time goes in v4:
time: 34 us; the launch traced here: 33.8 us
  Pallas kernels  31.3 us (92%)
  local copies, waits for them, and re-layouts  1.89 us (6%)
  between operations  0.65 us (2%)
    pallas_call x1, Pallas kernels, shards(): pl.pallas_call(functools.partial(kernel, src_count, row_count, tile_count...  31.3 us
    unnamed x4, local copies, waits for them, and re-layouts  1.89 us

profile of v4, /device:TPU:0, one launch (start us, length us, event | category | flops | bytes accessed | tf_op | source)
XLA Modules:
  0.0 33.8 jit_solution(498177690458329546)
XLA Ops:
  0.6 31.3 %shard_map.95 = (f32[1,32,256]{2,1,0:T(8,128)}, f32[3]{0:T(128)}) custom-call(bf16[2,256,512]{2,1,0:T(8,128)(2,1)} %constant.6.clone.wy_hbm, bf16[2,2,256,256]{3,2,1,0:T(8,128)(2,1)} %constant.7.clone.wx_hbm, bf16[2,2,256,256]{3,2,1,0:T(8,128)(2,1)} %constant.8.clone.wxt_hbm, f32[1,32,256]{2,1,0:T(8,128)} %mask_hbm.1, f32[1,32,256]{2,1,0:T(8,128)} %goal_hbm.1, ...), custom_call_target="tpu_custom_call" | custom-call | tf_op jit(solution)/shard_map/pallas_call | solution.py:610
  31.9 0.0 copy-start
  31.9 1.4 %copy.12 = f32[1,32,256]{2,1,0:T(8,128)} copy(f32[1,32,256]{2,1,0:T(8,128)} %get-tuple-element.4) | data formatting | bytes 65536
  33.3 0.0 copy-done
  33.3 0.5 %copy.13 = f32[3]{0:T(128)} copy(f32[3]{0:T(128)S(1)} %copy-done) | data formatting | bytes 24
Async XLA Ops:
  31.9 1.4 %copy-start = (f32[3]{0:T(128)S(1)}, f32[3]{0:T(128)}, u32[]{:S(2)}) copy-start(f32[3]{0:T(128)} %get-tuple-element.5) | copy-start | bytes 40
